TPU v7x, 128 devices: a whole 4x4x4 slice. The times are simulated.
128 devices in a mesh: row: 16 (over y, z), col: 8 (over x, core).
Axes of the slice: x: 4, y: 4, z: 4, core: 2. Of those that a mesh axis runs over, the one named last changes fastest.
Arguments:
- blocks: bfloat16 [16, 8, 128, 4096], P('row', 'col'), may hold values from -0.25 to 0.25
- block_row: int32 [16, 8, 128], P('row', 'col'), may hold values from 0 to 15
- block_col: int32 [16, 8, 128], P('row', 'col'), may hold values from 0 to 31
- counts: int32 [16, 8], P('row', 'col'), may hold values from 0 to 128, as said below
- vectors: float32 [256, 4096], P(('col', 'row')), may hold values from -6 to 6
- row_mass: float32 [256, 64], P(('row', 'col')), may hold values from 0.25 to 4
- col_mass: float32 [256, 64], P(('col', 'row')), may hold values from 0.25 to 4
Outputs:
- subspace: float32 [256, 4096], P(('col', 'row'))
Inputs may be any that keep to these rules, and one draw needn't show every extreme that they name: `counts`: in every row panel one tile uses all 128 slots; every other tile uses at most 8.
All inputs are finite; a program needn't handle non-finite values.
Results may differ from a plain program's by a relative error of at most 0.0085.
Values may be sent and summed in bfloat16 or wider, within the bound.
A program may use at most 64 MiB of HBM per device.

v0:
```python
import jax
import jax.numpy as jnp
from jax import lax
from jax.sharding import PartitionSpec as P

ITERS = 4


def rotate(projected, gram):
    lower = jnp.linalg.cholesky(gram)
    inverse = lax.linalg.triangular_solve(
        lower, jnp.eye(gram.shape[0], dtype=jnp.float32), left_side=True, lower=True
    )
    return jnp.einsum(
        "kl,bli->bki",
        inverse,
        projected,
        precision=lax.Precision.HIGHEST,
        preferred_element_type=jnp.float32,
    )


def local_gram(projected):
    return jnp.einsum(
        "bki,bli->kl",
        projected,
        projected,
        precision=lax.Precision.HIGHEST,
        preferred_element_type=jnp.float32,
    )


def per_device(blocks, block_row, block_col, counts, vectors, row_mass, col_mass):
    tile = blocks[0, 0]
    n_cap = tile.shape[0]
    bsize = row_mass.shape[1]
    vecs = vectors.shape[1] // bsize
    own = vectors.shape[0]
    n_row = lax.axis_size("row")
    n_col = lax.axis_size("col")
    row_panel = own * n_col
    col_panel = own * n_row
    total_boxes = float(own * bsize * n_row * n_col)
    rows_idx = block_row[0, 0]
    cols_idx = block_col[0, 0]
    live = jnp.arange(n_cap) < counts[0, 0]
    fwd_ids = jnp.where(live, rows_idx, row_panel)
    bwd_ids = jnp.where(live, cols_idx, col_panel)
    square = tile.reshape(n_cap, bsize, bsize)
    col_mass_panel = lax.all_gather(col_mass, "row", axis=0, tiled=True)
    row_mass_panel = lax.all_gather(row_mass, "col", axis=0, tiled=True)
    inv_col = 1.0 / jnp.sqrt(col_mass_panel)
    current = lax.all_gather(vectors, "row", axis=0, tiled=True).reshape(col_panel, vecs, bsize)
    for step in range(ITERS):
        scaled = (current * inv_col[:, None, :]).astype(jnp.bfloat16)
        forward_taken = jnp.take(scaled, cols_idx, axis=0)
        forward_product = jnp.einsum(
            "bij,bkj->bki", square, forward_taken, preferred_element_type=jnp.float32
        )
        forward_summed = jax.ops.segment_sum(forward_product, fwd_ids, num_segments=row_panel + 1)
        rows_sum = lax.psum(forward_summed[:row_panel], "col")
        weighted = (rows_sum * row_mass_panel[:, None, :]).astype(jnp.bfloat16)
        taken = jnp.take(weighted, rows_idx, axis=0)
        product = jnp.einsum("bij,bki->bkj", square, taken, preferred_element_type=jnp.float32)
        summed = jax.ops.segment_sum(product, bwd_ids, num_segments=col_panel + 1)
        cols_sum = lax.psum(summed[:col_panel], "row")
        projected = cols_sum * inv_col[:, None, :]
        gram = lax.psum(local_gram(projected), "col") / total_boxes
        current = rotate(projected, gram)
    me = lax.axis_index("row")
    mine = lax.dynamic_slice_in_dim(current, me * own, own, 0)
    return mine.reshape(own, vecs * bsize)


def solution(mesh):
    in_specs = (
        P("row", "col", None, None),
        P("row", "col", None),
        P("row", "col", None),
        P("row", "col"),
        P(("col", "row"), None),
        P(("row", "col"), None),
        P(("col", "row"), None),
    )
    out_specs = P(("col", "row"), None)
    return jax.shard_map(
        per_device, mesh=mesh, in_specs=in_specs, out_specs=out_specs, check_vma=False
    )
```

profile of v0, /device:TPU:0, one launch (start us, length us, event | category | flops | bytes accessed | tf_op | source)
XLA Modules:
  0.0 997.5 jit_solution(7439342869983005372)
XLA Ops:
  7.9 24.9 %all-gather.1 = f32[16,2,64]{2,1,0:T(2,128)S(1)} all-gather(f32[1,2,64]{2,1,0:T(2,128)} %bitcast.111), channel_id=1, replica_groups=mesh['row'=16,'col'=8] {'row'}, dimensions={0}, use_global_device_ids=true | all-gather | bytes 8704 | tf_op jit(solution)/shard_map/all_gather | solution.py:50
  32.8 23.5 %all-gather = f32[16,2,4096]{2,1,0:T(2,128)S(1)} all-gather(f32[1,2,4096]{2,1,0:T(2,128)} %bitcast.110), channel_id=1, replica_groups=mesh['row'=16,'col'=8] {'row'}, dimensions={0}, use_global_device_ids=true | all-gather | bytes 557056 | tf_op jit(solution)/shard_map/all_gather | solution.py:53
  58.6 3.0 copy.41
  65.8 4.8 fusion.14
  70.6 13.5 %scatter_fusion = f32[17,64,64]{2,1,0:T(8,128)S(1)} fusion(f32[17,64,64]{2,1,0:T(8,128)S(1)} %broadcast.82.clone.2, s32[128]{0:T(128)S(1)} %get-tuple-element.8, f32[128,64,64]{2,1,0:T(8,128)} %fusion.14), kind=kCustom, calls=%fused_computation.8 | custom fusion | flops 524288 | bytes 6291968 | tf_op jit(solution)/shard_map/scatter-add | solution.py:60
  85.1 10.7 %all-gather.2 = f32[8,2,64]{2,1,0:T(2,128)S(1)} all-gather(f32[1,2,64]{2,1,0:T(2,128)S(1)} %bitcast.112), channel_id=1, replica_groups=mesh['row'=16,'col'=8] {'col'}, dimensions={0}, use_global_device_ids=true | all-gather | bytes 4608 | tf_op jit(solution)/shard_map/all_gather | solution.py:51
  95.8 48.5 %all-reduce.9.cloned.1.call-done = f32[16,64,64]{2,1,0:T(8,128)} async-done(((f32[16,64,64]{2,1,0:T(8,128)}), f32[16,64,64]{2,1,0:T(8,128)}) %all-reduce.9.cloned.1.call-update) | async-done | bytes 262160 | tf_op jit(solution)/shard_map/psum | solution.py:61
  147.6 4.3 fusion.12
  152.0 13.5 %scatter_fusion.1 = f32[33,64,64]{2,1,0:T(8,128)S(1)} fusion(f32[33,64,64]{2,1,0:T(8,128)S(1)} %broadcast.81.clone.2, s32[128]{0:T(128)S(1)} %get-tuple-element.6, f32[128,64,64]{2,1,0:T(8,128)} %fusion.12), kind=kCustom, calls=%fused_computation.9 | custom fusion | flops 524288 | bytes 6291968 | tf_op jit(solution)/shard_map/scatter-add | solution.py:65
  166.7 86.6 %all-reduce.11.cloned.1.call-done = f32[32,64,64]{2,1,0:T(8,128)} async-done(((f32[32,64,64]{2,1,0:T(8,128)}), f32[32,64,64]{2,1,0:T(8,128)}) %all-reduce.11.cloned.1.call-update) | async-done | bytes 524304 | tf_op jit(solution)/shard_map/psum | solution.py:66
  253.2 2.7 convolution_bitcast_fusion.7
  256.0 24.8 %psum.86 = f32[64,64]{0,1:T(8,128)S(1)} all-reduce(f32[64,64]{0,1:T(8,128)S(1)} %convolution_bitcast_fusion.7), channel_id=1, replica_groups=mesh['row'=16,'col'=8] {'col'}, use_global_device_ids=true, to_apply=%region_4.7 | all-reduce | flops 4096 | bytes 32768 | tf_op jit(solution)/shard_map/psum | solution.py:68
  280.9 5.8 cholesky.74
  288.1 4.9 custom-call.8
  293.2 2.8 fusion.29
  297.3 2.1 gather_fusion.2
  299.5 4.8 fusion.10
  304.3 13.5 %scatter_fusion.2 = f32[17,64,64]{2,1,0:T(8,128)S(1)} fusion(f32[17,64,64]{2,1,0:T(8,128)S(1)} %broadcast.82.clone.1, s32[128]{0:T(128)S(1)} %get-tuple-element.8, f32[128,64,64]{2,1,0:T(8,128)} %fusion.10), kind=kCustom, calls=%fused_computation.10 | custom fusion | flops 524288 | bytes 6291968 | tf_op jit(solution)/shard_map/scatter-add | solution.py:60
  318.7 57.4 %all-reduce.13.cloned.1.call-done = f32[16,64,64]{2,1,0:T(8,128)} async-done(((f32[16,64,64]{2,1,0:T(8,128)}), f32[16,64,64]{2,1,0:T(8,128)}) %all-reduce.13.cloned.1.call-update) | async-done | bytes 262160 | tf_op jit(solution)/shard_map/psum | solution.py:61
  379.3 4.3 fusion.8
  383.7 13.5 %scatter_fusion.3 = f32[33,64,64]{2,1,0:T(8,128)S(1)} fusion(f32[33,64,64]{2,1,0:T(8,128)S(1)} %broadcast.81.clone.1, s32[128]{0:T(128)S(1)} %get-tuple-element.6, f32[128,64,64]{2,1,0:T(8,128)} %fusion.8), kind=kCustom, calls=%fused_computation.11 | custom fusion | flops 524288 | bytes 6291968 | tf_op jit(solution)/shard_map/scatter-add | solution.py:65
  398.4 86.6 %all-reduce.15.cloned.1.call-done = f32[32,64,64]{2,1,0:T(8,128)} async-done(((f32[32,64,64]{2,1,0:T(8,128)}), f32[32,64,64]{2,1,0:T(8,128)}) %all-reduce.15.cloned.1.call-update) | async-done | bytes 524304 | tf_op jit(solution)/shard_map/psum | solution.py:66
  485.1 2.7 convolution_bitcast_fusion.5
  487.8 24.4 %psum.89 = f32[64,64]{0,1:T(8,128)S(1)} all-reduce(f32[64,64]{0,1:T(8,128)S(1)} %convolution_bitcast_fusion.5), channel_id=1, replica_groups=mesh['row'=16,'col'=8] {'col'}, use_global_device_ids=true, to_apply=%region_11.16 | all-reduce | flops 4096 | bytes 32768 | tf_op jit(solution)/shard_map/psum | solution.py:68
  512.3 5.8 cholesky.85
  519.5 4.9 custom-call.9
  524.7 2.8 fusion.28
  530.9 4.8 fusion.6
  535.8 13.5 %scatter_fusion.4 = f32[17,64,64]{2,1,0:T(8,128)S(1)} fusion(f32[17,64,64]{2,1,0:T(8,128)S(1)} %broadcast.82.clone, s32[128]{0:T(128)S(1)} %get-tuple-element.8, f32[128,64,64]{2,1,0:T(8,128)} %fusion.6), kind=kCustom, calls=%fused_computation.12 | custom fusion | flops 524288 | bytes 6291968 | tf_op jit(solution)/shard_map/scatter-add | solution.py:60
  550.2 57.4 %all-reduce.17.cloned.1.call-done = f32[16,64,64]{2,1,0:T(8,128)} async-done(((f32[16,64,64]{2,1,0:T(8,128)}), f32[16,64,64]{2,1,0:T(8,128)}) %all-reduce.17.cloned.1.call-update) | async-done | bytes 262160 | tf_op jit(solution)/shard_map/psum | solution.py:61
  610.8 4.3 fusion.4
  615.2 13.5 %scatter_fusion.5 = f32[33,64,64]{2,1,0:T(8,128)S(1)} fusion(f32[33,64,64]{2,1,0:T(8,128)S(1)} %broadcast.81.clone, s32[128]{0:T(128)S(1)} %get-tuple-element.6, f32[128,64,64]{2,1,0:T(8,128)} %fusion.4), kind=kCustom, calls=%fused_computation.13 | custom fusion | flops 524288 | bytes 6291968 | tf_op jit(solution)/shard_map/scatter-add | solution.py:65
  629.9 86.6 %all-reduce.19.cloned.1.call-done = f32[32,64,64]{2,1,0:T(8,128)} async-done(((f32[32,64,64]{2,1,0:T(8,128)}), f32[32,64,64]{2,1,0:T(8,128)}) %all-reduce.19.cloned.1.call-update) | async-done | bytes 524304 | tf_op jit(solution)/shard_map/psum | solution.py:66
  716.6 2.7 convolution_bitcast_fusion.3
  719.3 24.5 %psum.92 = f32[64,64]{0,1:T(8,128)S(1)} all-reduce(f32[64,64]{0,1:T(8,128)S(1)} %convolution_bitcast_fusion.3), channel_id=1, replica_groups=mesh['row'=16,'col'=8] {'col'}, use_global_device_ids=true, to_apply=%region_16.21 | all-reduce | flops 4096 | bytes 32768 | tf_op jit(solution)/shard_map/psum | solution.py:68
  743.9 5.8 cholesky.96
  751.1 4.9 custom-call.10
  756.2 2.8 fusion.27
  762.5 4.8 fusion.2
  767.3 13.5 %scatter_fusion.6 = f32[17,64,64]{2,1,0:T(8,128)S(1)} fusion(f32[17,64,64]{2,1,0:T(8,128)S(1)} %broadcast.82, s32[128]{0:T(128)S(1)} %get-tuple-element.8, f32[128,64,64]{2,1,0:T(8,128)} %fusion.2), kind=kCustom, calls=%fused_computation.14 | custom fusion | flops 524288 | bytes 6291968 | tf_op jit(solution)/shard_map/scatter-add | solution.py:60
  781.7 57.4 %all-reduce.21.cloned.1.call-done = f32[16,64,64]{2,1,0:T(8,128)} async-done(((f32[16,64,64]{2,1,0:T(8,128)}), f32[16,64,64]{2,1,0:T(8,128)}) %all-reduce.21.cloned.1.call-update) | async-done | bytes 262160 | tf_op jit(solution)/shard_map/psum | solution.py:61
  842.3 4.3 fusion
  846.7 13.5 %scatter_fusion.7 = f32[33,64,64]{2,1,0:T(8,128)S(1)} fusion(f32[33,64,64]{2,1,0:T(8,128)S(1)} %broadcast.81, s32[128]{0:T(128)S(1)} %get-tuple-element.6, f32[128,64,64]{2,1,0:T(8,128)} %fusion), kind=kCustom, calls=%fused_computation.15 | custom fusion | flops 524288 | bytes 6291968 | tf_op jit(solution)/shard_map/scatter-add | solution.py:65
  861.4 86.7 %all-reduce.23.cloned.1.call-done = f32[32,64,64]{2,1,0:T(8,128)} async-done(((f32[32,64,64]{2,1,0:T(8,128)}), f32[32,64,64]{2,1,0:T(8,128)}) %all-reduce.23.cloned.1.call-update) | async-done | bytes 524304 | tf_op jit(solution)/shard_map/psum | solution.py:66
  948.1 2.7 convolution_bitcast_fusion.1
  950.8 24.5 %psum.95 = f32[64,64]{0,1:T(8,128)S(1)} all-reduce(f32[64,64]{0,1:T(8,128)S(1)} %convolution_bitcast_fusion.1), channel_id=1, replica_groups=mesh['row'=16,'col'=8] {'col'}, use_global_device_ids=true, to_apply=%region_21.26 | all-reduce | flops 4096 | bytes 32768 | tf_op jit(solution)/shard_map/psum | solution.py:68
  975.4 5.8 cholesky.107
  982.6 4.9 custom-call.11
  (105 shorter events, 46.7 us)
Async XLA Ops:
  6.5 51.4 %copy-start.4 = (bf16[1,1,128,4096]{3,2,1,0:T(8,128)(2,1)S(1)}, bf16[1,1,128,4096]{3,2,1,0:T(8,128)(2,1)}, u32[]{:S(2)}) copy-start(bf16[1,1,128,4096]{3,2,1,0:T(8,128)(2,1)} %param.14) | copy-start | bytes 3145732
  6.5 137.8 %all-reduce.9.cloned.1.call-start = ((), (), s32[]{:S(2)}) async-start(), calls=%async_computation | async-start | bytes 1048576 | tf_op jit(solution)/shard_map/psum | solution.py:61
  63.6 2.2 copy-start.6
  63.6 2.2 copy-start.7
  70.6 14.5 %copy-start.5 = (f32[2,64]{1,0:T(2,128)S(1)}, f32[2,64]{1,0:T(2,128)}, u32[]{:S(2)}) copy-start(f32[2,64]{1,0:T(2,128)} %param.19) | copy-start | bytes 1540
  85.0 168.2 %all-reduce.11.cloned.1.call-start = ((), (), s32[]{:S(2)}) async-start(), calls=%async_computation.1 | async-start | bytes 2097152 | tf_op jit(solution)/shard_map/psum | solution.py:66
  166.6 209.5 %all-reduce.13.cloned.1.call-start = ((), (), s32[]{:S(2)}) async-start(), calls=%async_computation.2 | async-start | bytes 1048576 | tf_op jit(solution)/shard_map/psum | solution.py:61
  253.2 40.0 %copy-start.1 = (f32[32,64,64]{2,1,0:T(8,128)S(1)}, f32[32,64,64]{2,1,0:T(8,128)}, u32[]{:S(2)}) copy-start(f32[32,64,64]{2,1,0:T(8,128)} %all-reduce.11.cloned.1.call-done) | copy-start | bytes 1572868
  318.7 166.4 %all-reduce.15.cloned.1.call-start = ((), (), s32[]{:S(2)}) async-start(), calls=%async_computation.3 | async-start | bytes 2097152 | tf_op jit(solution)/shard_map/psum | solution.py:66
  398.4 209.2 %all-reduce.17.cloned.1.call-start = ((), (), s32[]{:S(2)}) async-start(), calls=%async_computation.4 | async-start | bytes 1048576 | tf_op jit(solution)/shard_map/psum | solution.py:61
  485.1 39.6 %copy-start.2 = (f32[32,64,64]{2,1,0:T(8,128)S(1)}, f32[32,64,64]{2,1,0:T(8,128)}, u32[]{:S(2)}) copy-start(f32[32,64,64]{2,1,0:T(8,128)} %all-reduce.15.cloned.1.call-done) | copy-start | bytes 1572868
  550.1 166.4 %all-reduce.19.cloned.1.call-start = ((), (), s32[]{:S(2)}) async-start(), calls=%async_computation.5 | async-start | bytes 2097152 | tf_op jit(solution)/shard_map/psum | solution.py:66
  629.9 209.2 %all-reduce.21.cloned.1.call-start = ((), (), s32[]{:S(2)}) async-start(), calls=%async_computation.6 | async-start | bytes 1048576 | tf_op jit(solution)/shard_map/psum | solution.py:61
  716.6 39.7 %copy-start.3 = (f32[32,64,64]{2,1,0:T(8,128)S(1)}, f32[32,64,64]{2,1,0:T(8,128)}, u32[]{:S(2)}) copy-start(f32[32,64,64]{2,1,0:T(8,128)} %all-reduce.19.cloned.1.call-done) | copy-start | bytes 1572868
  781.7 166.4 %all-reduce.23.cloned.1.call-start = ((), (), s32[]{:S(2)}) async-start(), calls=%async_computation.7 | async-start | bytes 2097152 | tf_op jit(solution)/shard_map/psum | solution.py:66
  948.1 39.7 %copy-start = (f32[32,64,64]{2,1,0:T(8,128)S(1)}, f32[32,64,64]{2,1,0:T(8,128)}, u32[]{:S(2)}) copy-start(f32[32,64,64]{2,1,0:T(8,128)} %all-reduce.23.cloned.1.call-done) | copy-start | bytes 1572868
Sparse Core Ops, SparseCore 0:
  85.2 59.1 all-reduce.8
  166.7 86.4 all-reduce.10
  318.8 57.2 all-reduce.12
  398.5 86.4 all-reduce.14
  550.3 57.2 all-reduce.16
  630.0 86.5 all-reduce.18
  781.8 57.2 all-reduce.20
  861.6 86.4 all-reduce.22
where the time goes:
time: 1010 us; the launch traced here: 998 us
  waiting for transfers between devices  567 us (56%)
  other arithmetic  164 us (16%)
  blocking collectives  157 us (16%)
  matrix products  58.3 us (6%)
  local copies, waits for them, and re-layouts  36 us (4%)
  between operations  14.9 us (1%)
    psum x4, waiting for transfers between devices, per_device(): cols_sum = lax.psum(summed[:col_panel], 'row')  346 us
    psum x4, waiting for transfers between devices, per_device(): rows_sum = lax.psum(forward_summed[:row_panel], 'col')  221 us
    psum x4, blocking collectives, per_device(): gram = lax.psum(local_gram(projected), 'col') / total_boxes  98.2 us
    scatter-add x4, other arithmetic, per_device(): summed = jax.ops.segment_sum(product, bwd_ids, num_segments=col_panel + 1)  54.1 us
    scatter-add x4, other arithmetic, per_device(): jax.ops.segment_sum(forward_product, fwd_ids, num_segments=row_panel + 1)  54 us
    another operation x12, other arithmetic, rotate(): lower = jnp.linalg.cholesky(gram)  26.1 us
    all_gather x1, blocking collectives, per_device(): col_mass_panel = lax.all_gather(col_mass, 'row', axis=0, tiled=True)  24.9 us
    all_gather x1, blocking collectives, per_device(): lax.all_gather(vectors, 'row', axis=0, tiled=True)  23.5 us
  transfers between devices with their start and end apart: 8, of which 8 were waited for; matrix products, arithmetic and copies ran while one was open for 0% of the time, Pallas kernels for 0%

commit v1 on v0

--- a/solution.py
+++ b/solution.py
@@ -4,6 +4,16 @@
 from jax.sharding import PartitionSpec as P
 
 ITERS = 4
+
+
+def turned_line(value, mesh_axis, along):
+    peers = lax.axis_size(mesh_axis)
+    current, pieces = (value, [value])
+    for _ in range(peers - 1):
+        current = lax.ppermute(current, mesh_axis, [(i, (i + 1) % peers) for i in range(peers)])
+        pieces.insert(0, current)
+    merged = jnp.concatenate(pieces, axis=along)
+    return jnp.roll(merged, (lax.axis_index(mesh_axis) + 1) * value.shape[along], axis=along)
 
 
 def rotate(projected, gram):
@@ -47,7 +57,7 @@
     fwd_ids = jnp.where(live, rows_idx, row_panel)
     bwd_ids = jnp.where(live, cols_idx, col_panel)
     square = tile.reshape(n_cap, bsize, bsize)
-    col_mass_panel = lax.all_gather(col_mass, "row", axis=0, tiled=True)
+    col_mass_panel = turned_line(col_mass, "row", 0)
     row_mass_panel = lax.all_gather(row_mass, "col", axis=0, tiled=True)
     inv_col = 1.0 / jnp.sqrt(col_mass_panel)
     current = lax.all_gather(vectors, "row", axis=0, tiled=True).reshape(col_panel, vecs, bsize)

time: 1010 us -> 1080 us (1.069)
  waiting for transfers between devices: 567 us -> 654 us
  blocking collectives: 157 us -> 133 us
    ppermute x0 -> x15, waiting for transfers between devices: none -> 86.1 us  [turned_line(): lax.ppermute(current, mesh_axis, [(i, (i + 1) % peers) for i in range(pee...]
    all_gather x1 -> x0, blocking collectives: 24.9 us -> none  [per_device(): col_mass_panel = lax.all_gather(col_mass, 'row', axis=0, tiled=True)]
  transfers between devices with their start and end apart: 8 -> 23, of which waited for: 8 -> 22; matrix products, arithmetic and copies ran while one was open for 0% -> 1% of each run, Pallas kernels for 0% -> 0%
where the time goes in v1:
time: 1080 us; the launch traced here: 1060 us
  waiting for transfers between devices  654 us (61%)
  other arithmetic  165 us (15%)
  blocking collectives  133 us (12%)
  matrix products  58.3 us (5%)
  local copies, waits for them, and re-layouts  36.2 us (3%)
  between operations  14.9 us (1%)
    psum x4, waiting for transfers between devices, per_device(): cols_sum = lax.psum(summed[:col_panel], 'row')  346 us
    psum x4, waiting for transfers between devices, per_device(): rows_sum = lax.psum(forward_summed[:row_panel], 'col')  221 us
    psum x4, blocking collectives, per_device(): gram = lax.psum(local_gram(projected), 'col') / total_boxes  97.4 us
    ppermute x15, waiting for transfers between devices, turned_line(): lax.ppermute(current, mesh_axis, [(i, (i + 1) % peers) for i in range(pee...  86.1 us
    scatter-add x4, other arithmetic, per_device(): summed = jax.ops.segment_sum(product, bwd_ids, num_segments=col_panel + 1)  54.1 us
    scatter-add x4, other arithmetic, per_device(): jax.ops.segment_sum(forward_product, fwd_ids, num_segments=row_panel + 1)  54 us
    another operation x12, other arithmetic, rotate(): lower = jnp.linalg.cholesky(gram)  26.1 us
    all_gather x1, blocking collectives, per_device(): lax.all_gather(vectors, 'row', axis=0, tiled=True)  24.4 us
  transfers between devices with their start and end apart: 23, of which 22 were waited for; matrix products, arithmetic and copies ran while one was open for 1% of the time, Pallas kernels for 0%

profile of v1, /device:TPU:0, one launch (start us, length us, event | category | flops | bytes accessed | tf_op | source)
XLA Modules:
  0.0 1064.5 jit_solution(1984990714526070705)
XLA Ops:
  8.5 6.3 collective-permute-done
  14.9 6.9 collective-permute-done.1
  21.8 6.9 collective-permute-done.2
  28.6 6.9 collective-permute-done.3
  35.5 6.9 collective-permute-done.4
  43.1 6.2 collective-permute-done.5
  50.0 6.2 collective-permute-done.6
  56.9 6.2 collective-permute-done.7
  63.8 6.2 collective-permute-done.8
  70.6 6.2 collective-permute-done.9
  76.9 24.4 %all-gather = f32[16,2,4096]{2,1,0:T(2,128)S(1)} all-gather(f32[1,2,4096]{2,1,0:T(2,128)} %bitcast.99), channel_id=1, replica_groups=mesh['row'=16,'col'=8] {'row'}, dimensions={0}, use_global_device_ids=true | all-gather | bytes 557056 | tf_op jit(solution)/shard_map/all_gather | solution.py:63
  102.5 5.7 collective-permute-done.11
  108.3 6.9 collective-permute-done.12
  115.1 6.9 collective-permute-done.13
  132.6 4.8 fusion.14
  137.5 13.5 %scatter_fusion = f32[17,64,64]{2,1,0:T(8,128)S(1)} fusion(f32[17,64,64]{2,1,0:T(8,128)S(1)} %broadcast.83.clone.2, s32[128]{0:T(128)S(1)} %get-tuple-element.8, f32[128,64,64]{2,1,0:T(8,128)} %fusion.14), kind=kCustom, calls=%fused_computation.8 | custom fusion | flops 524288 | bytes 6291968 | tf_op jit(solution)/shard_map/scatter-add | solution.py:70
  151.9 10.8 %all-gather.1 = f32[8,2,64]{2,1,0:T(2,128)S(1)} all-gather(f32[1,2,64]{2,1,0:T(2,128)S(1)} %bitcast.100), channel_id=1, replica_groups=mesh['row'=16,'col'=8] {'col'}, dimensions={0}, use_global_device_ids=true | all-gather | bytes 4608 | tf_op jit(solution)/shard_map/all_gather | solution.py:61
  162.8 49.4 %all-reduce.9.cloned.1.call-done = f32[16,64,64]{2,1,0:T(8,128)} async-done(((f32[16,64,64]{2,1,0:T(8,128)}), f32[16,64,64]{2,1,0:T(8,128)}) %all-reduce.9.cloned.1.call-update) | async-done | bytes 262160 | tf_op jit(solution)/shard_map/psum | solution.py:71
  215.4 4.3 fusion.12
  219.8 13.5 %scatter_fusion.1 = f32[33,64,64]{2,1,0:T(8,128)S(1)} fusion(f32[33,64,64]{2,1,0:T(8,128)S(1)} %broadcast.82.clone.2, s32[128]{0:T(128)S(1)} %get-tuple-element.6, f32[128,64,64]{2,1,0:T(8,128)} %fusion.12), kind=kCustom, calls=%fused_computation.9 | custom fusion | flops 524288 | bytes 6291968 | tf_op jit(solution)/shard_map/scatter-add | solution.py:75
  234.5 86.6 %all-reduce.11.cloned.1.call-done = f32[32,64,64]{2,1,0:T(8,128)} async-done(((f32[32,64,64]{2,1,0:T(8,128)}), f32[32,64,64]{2,1,0:T(8,128)}) %all-reduce.11.cloned.1.call-update) | async-done | bytes 524304 | tf_op jit(solution)/shard_map/psum | solution.py:76
  323.9 24.1 %psum.86 = f32[64,64]{0,1:T(8,128)S(1)} all-reduce(f32[64,64]{0,1:T(8,128)S(1)} %convolution_bitcast_fusion.7), channel_id=1, replica_groups=mesh['row'=16,'col'=8] {'col'}, use_global_device_ids=true, to_apply=%region_4.7 | all-reduce | flops 4096 | bytes 32768 | tf_op jit(solution)/shard_map/psum | solution.py:78
  348.1 5.8 cholesky.74
  355.3 4.9 custom-call.8
  366.7 4.8 fusion.10
  371.5 13.5 %scatter_fusion.2 = f32[17,64,64]{2,1,0:T(8,128)S(1)} fusion(f32[17,64,64]{2,1,0:T(8,128)S(1)} %broadcast.83.clone.1, s32[128]{0:T(128)S(1)} %get-tuple-element.8, f32[128,64,64]{2,1,0:T(8,128)} %fusion.10), kind=kCustom, calls=%fused_computation.10 | custom fusion | flops 524288 | bytes 6291968 | tf_op jit(solution)/shard_map/scatter-add | solution.py:70
  386.0 57.4 %all-reduce.13.cloned.1.call-done = f32[16,64,64]{2,1,0:T(8,128)} async-done(((f32[16,64,64]{2,1,0:T(8,128)}), f32[16,64,64]{2,1,0:T(8,128)}) %all-reduce.13.cloned.1.call-update) | async-done | bytes 262160 | tf_op jit(solution)/shard_map/psum | solution.py:71
  451.0 13.5 %scatter_fusion.3 = f32[33,64,64]{2,1,0:T(8,128)S(1)} fusion(f32[33,64,64]{2,1,0:T(8,128)S(1)} %broadcast.82.clone.1, s32[128]{0:T(128)S(1)} %get-tuple-element.6, f32[128,64,64]{2,1,0:T(8,128)} %fusion.8), kind=kCustom, calls=%fused_computation.11 | custom fusion | flops 524288 | bytes 6291968 | tf_op jit(solution)/shard_map/scatter-add | solution.py:75
  465.9 86.4 %all-reduce.15.cloned.1.call-done = f32[32,64,64]{2,1,0:T(8,128)} async-done(((f32[32,64,64]{2,1,0:T(8,128)}), f32[32,64,64]{2,1,0:T(8,128)}) %all-reduce.15.cloned.1.call-update) | async-done | bytes 524304 | tf_op jit(solution)/shard_map/psum | solution.py:76
  555.0 24.1 %psum.89 = f32[64,64]{0,1:T(8,128)S(1)} all-reduce(f32[64,64]{0,1:T(8,128)S(1)} %convolution_bitcast_fusion.5), channel_id=1, replica_groups=mesh['row'=16,'col'=8] {'col'}, use_global_device_ids=true, to_apply=%region_11.16 | all-reduce | flops 4096 | bytes 32768 | tf_op jit(solution)/shard_map/psum | solution.py:78
  579.3 5.8 cholesky.85
  586.5 4.9 custom-call.9
  597.9 4.8 fusion.6
  602.7 13.5 %scatter_fusion.4 = f32[17,64,64]{2,1,0:T(8,128)S(1)} fusion(f32[17,64,64]{2,1,0:T(8,128)S(1)} %broadcast.83.clone, s32[128]{0:T(128)S(1)} %get-tuple-element.8, f32[128,64,64]{2,1,0:T(8,128)} %fusion.6), kind=kCustom, calls=%fused_computation.12 | custom fusion | flops 524288 | bytes 6291968 | tf_op jit(solution)/shard_map/scatter-add | solution.py:70
  617.1 57.4 %all-reduce.17.cloned.1.call-done = f32[16,64,64]{2,1,0:T(8,128)} async-done(((f32[16,64,64]{2,1,0:T(8,128)}), f32[16,64,64]{2,1,0:T(8,128)}) %all-reduce.17.cloned.1.call-update) | async-done | bytes 262160 | tf_op jit(solution)/shard_map/psum | solution.py:71
  682.1 13.5 %scatter_fusion.5 = f32[33,64,64]{2,1,0:T(8,128)S(1)} fusion(f32[33,64,64]{2,1,0:T(8,128)S(1)} %broadcast.82.clone, s32[128]{0:T(128)S(1)} %get-tuple-element.6, f32[128,64,64]{2,1,0:T(8,128)} %fusion.4), kind=kCustom, calls=%fused_computation.13 | custom fusion | flops 524288 | bytes 6291968 | tf_op jit(solution)/shard_map/scatter-add | solution.py:75
  696.8 86.6 %all-reduce.19.cloned.1.call-done = f32[32,64,64]{2,1,0:T(8,128)} async-done(((f32[32,64,64]{2,1,0:T(8,128)}), f32[32,64,64]{2,1,0:T(8,128)}) %all-reduce.19.cloned.1.call-update) | async-done | bytes 524304 | tf_op jit(solution)/shard_map/psum | solution.py:76
  786.2 24.7 %psum.92 = f32[64,64]{0,1:T(8,128)S(1)} all-reduce(f32[64,64]{0,1:T(8,128)S(1)} %convolution_bitcast_fusion.3), channel_id=1, replica_groups=mesh['row'=16,'col'=8] {'col'}, use_global_device_ids=true, to_apply=%region_16.21 | all-reduce | flops 4096 | bytes 32768 | tf_op jit(solution)/shard_map/psum | solution.py:78
  811.0 5.8 cholesky.96
  818.2 4.9 custom-call.10
  829.6 4.8 fusion.2
  834.4 13.5 %scatter_fusion.6 = f32[17,64,64]{2,1,0:T(8,128)S(1)} fusion(f32[17,64,64]{2,1,0:T(8,128)S(1)} %broadcast.83, s32[128]{0:T(128)S(1)} %get-tuple-element.8, f32[128,64,64]{2,1,0:T(8,128)} %fusion.2), kind=kCustom, calls=%fused_computation.14 | custom fusion | flops 524288 | bytes 6291968 | tf_op jit(solution)/shard_map/scatter-add | solution.py:70
  848.8 57.4 %all-reduce.21.cloned.1.call-done = f32[16,64,64]{2,1,0:T(8,128)} async-done(((f32[16,64,64]{2,1,0:T(8,128)}), f32[16,64,64]{2,1,0:T(8,128)}) %all-reduce.21.cloned.1.call-update) | async-done | bytes 262160 | tf_op jit(solution)/shard_map/psum | solution.py:71
  913.8 13.5 %scatter_fusion.7 = f32[33,64,64]{2,1,0:T(8,128)S(1)} fusion(f32[33,64,64]{2,1,0:T(8,128)S(1)} %broadcast.82, s32[128]{0:T(128)S(1)} %get-tuple-element.6, f32[128,64,64]{2,1,0:T(8,128)} %fusion), kind=kCustom, calls=%fused_computation.15 | custom fusion | flops 524288 | bytes 6291968 | tf_op jit(solution)/shard_map/scatter-add | solution.py:75
  928.6 86.6 %all-reduce.23.cloned.1.call-done = f32[32,64,64]{2,1,0:T(8,128)} async-done(((f32[32,64,64]{2,1,0:T(8,128)}), f32[32,64,64]{2,1,0:T(8,128)}) %all-reduce.23.cloned.1.call-update) | async-done | bytes 524304 | tf_op jit(solution)/shard_map/psum | solution.py:76
  1017.9 24.4 %psum.95 = f32[64,64]{0,1:T(8,128)S(1)} all-reduce(f32[64,64]{0,1:T(8,128)S(1)} %convolution_bitcast_fusion.1), channel_id=1, replica_groups=mesh['row'=16,'col'=8] {'col'}, use_global_device_ids=true, to_apply=%region_21.26 | all-reduce | flops 4096 | bytes 32768 | tf_op jit(solution)/shard_map/psum | solution.py:78
  1042.5 5.8 cholesky.107
  1049.7 4.9 custom-call.11
  (135 shorter events, 90.3 us)
Async XLA Ops:
  6.5 117.1 %copy-start.4 = (bf16[1,1,128,4096]{3,2,1,0:T(8,128)(2,1)S(1)}, bf16[1,1,128,4096]{3,2,1,0:T(8,128)(2,1)}, u32[]{:S(2)}) copy-start(bf16[1,1,128,4096]{3,2,1,0:T(8,128)(2,1)} %param.14) | copy-start | bytes 3145732
  6.5 205.6 %all-reduce.9.cloned.1.call-start = ((), (), s32[]{:S(2)}) async-start(), calls=%async_computation | async-start | bytes 1048576 | tf_op jit(solution)/shard_map/psum | solution.py:71
  6.5 8.3 collective-permute-start
  14.9 6.9 collective-permute-start.1
  21.8 6.9 collective-permute-start.2
  28.6 6.9 collective-permute-start.3
  35.5 6.9 collective-permute-start.4
  42.4 6.9 collective-permute-start.5
  49.3 6.9 collective-permute-start.6
  56.2 6.9 collective-permute-start.7
  63.1 6.9 collective-permute-start.8
  70.0 6.9 collective-permute-start.9
  76.9 24.4 %collective-permute-start.10 = (f32[2,64]{1,0:T(2,128)S(1)}, f32[2,64]{1,0:T(2,128)S(1)}, u32[]{:S(2)}, u32[]{:S(2)}) collective-permute-start(f32[2,64]{1,0:T(2,128)S(1)} %collective-permute-done.9), channel_id=1, source_target_pairs={{0,8},{8,16},{16,24},{24,32},{32,40},{40,48},{48,56},{56,64},{64,7... | collective-permute-start | bytes 1544 | tf_op jit(solution)/shard_map/ppermute | solution.py:13
  101.3 7.0 collective-permute-start.11
  108.2 6.9 collective-permute-start.12
  115.1 6.9 collective-permute-start.13
  122.0 6.9 collective-permute-start.14
  124.3 4.6 copy-start.5
  137.4 14.5 %copy-start.7 = (s32[1,1,128]{2,1,0:T(1,128)S(1)}, s32[1,1,128]{2,1,0:T(1,128)}, u32[]{:S(2)}) copy-start(s32[1,1,128]{2,1,0:T(1,128)} %param.15) | copy-start | bytes 1540
  137.5 14.5 %copy-start.6 = (f32[2,64]{1,0:T(2,128)S(1)}, f32[2,64]{1,0:T(2,128)}, u32[]{:S(2)}) copy-start(f32[2,64]{1,0:T(2,128)} %param.19) | copy-start | bytes 1540
  151.9 169.2 %all-reduce.11.cloned.1.call-start = ((), (), s32[]{:S(2)}) async-start(), calls=%async_computation.1 | async-start | bytes 2097152 | tf_op jit(solution)/shard_map/psum | solution.py:76
  234.5 208.9 %all-reduce.13.cloned.1.call-start = ((), (), s32[]{:S(2)}) async-start(), calls=%async_computation.2 | async-start | bytes 1048576 | tf_op jit(solution)/shard_map/psum | solution.py:71
  321.1 39.3 %copy-start.1 = (f32[32,64,64]{2,1,0:T(8,128)S(1)}, f32[32,64,64]{2,1,0:T(8,128)}, u32[]{:S(2)}) copy-start(f32[32,64,64]{2,1,0:T(8,128)} %all-reduce.11.cloned.1.call-done) | copy-start | bytes 1572868
  385.9 166.4 %all-reduce.15.cloned.1.call-start = ((), (), s32[]{:S(2)}) async-start(), calls=%async_computation.3 | async-start | bytes 2097152 | tf_op jit(solution)/shard_map/psum | solution.py:76
  465.6 208.9 %all-reduce.17.cloned.1.call-start = ((), (), s32[]{:S(2)}) async-start(), calls=%async_computation.4 | async-start | bytes 1048576 | tf_op jit(solution)/shard_map/psum | solution.py:71
  552.3 39.3 %copy-start.2 = (f32[32,64,64]{2,1,0:T(8,128)S(1)}, f32[32,64,64]{2,1,0:T(8,128)}, u32[]{:S(2)}) copy-start(f32[32,64,64]{2,1,0:T(8,128)} %all-reduce.15.cloned.1.call-done) | copy-start | bytes 1572868
  617.1 166.4 %all-reduce.19.cloned.1.call-start = ((), (), s32[]{:S(2)}) async-start(), calls=%async_computation.5 | async-start | bytes 2097152 | tf_op jit(solution)/shard_map/psum | solution.py:76
  696.8 209.4 %all-reduce.21.cloned.1.call-start = ((), (), s32[]{:S(2)}) async-start(), calls=%async_computation.6 | async-start | bytes 1048576 | tf_op jit(solution)/shard_map/psum | solution.py:71
  783.5 39.9 %copy-start.3 = (f32[32,64,64]{2,1,0:T(8,128)S(1)}, f32[32,64,64]{2,1,0:T(8,128)}, u32[]{:S(2)}) copy-start(f32[32,64,64]{2,1,0:T(8,128)} %all-reduce.19.cloned.1.call-done) | copy-start | bytes 1572868
  848.8 166.4 %all-reduce.23.cloned.1.call-start = ((), (), s32[]{:S(2)}) async-start(), calls=%async_computation.7 | async-start | bytes 2097152 | tf_op jit(solution)/shard_map/psum | solution.py:76
  1015.2 39.6 %copy-start = (f32[32,64,64]{2,1,0:T(8,128)S(1)}, f32[32,64,64]{2,1,0:T(8,128)}, u32[]{:S(2)}) copy-start(f32[32,64,64]{2,1,0:T(8,128)} %all-reduce.23.cloned.1.call-done) | copy-start | bytes 1572868
Sparse Core Ops, SparseCore 0:
  152.0 60.1 all-reduce.8
  234.6 86.4 all-reduce.10
  386.0 57.2 all-reduce.12
  465.8 86.4 all-reduce.14
  617.2 57.2 all-reduce.16
  696.9 86.5 all-reduce.18
  848.9 57.2 all-reduce.20
  928.7 86.4 all-reduce.22
